TPU v7x, 32 devices: a whole 2x2x4 slice. The times are simulated.
32 devices in a mesh: work: 8 (over z, y), firm: 4 (over x, core).
Axes of the slice: x: 2, y: 2, z: 4, core: 2. Of those that a mesh axis runs over, the one named last changes fastest.
Arguments:
- worker_feat: bfloat16 [64, 16384], P('firm', 'work'), may hold values from -4 to 4
- firm_feat: bfloat16 [64, 16384], P('work', 'firm'), may hold values from -1.75 to 1.75
- worker_pot: float32 [16384], P('work'), may hold values from -1 to 1
- firm_pot: float32 [16384], P('firm'), may hold values from -1 to 1
- worker_caps: int32 [16384], P('work'), may hold values from 1 to 5
- firm_caps: int32 [16384], P('firm'), may hold values from 1 to 5
Outputs:
- step_workers: float32 [16384], P('work')
- step_firms: float32 [16384], P('firm')
All inputs are finite; a program needn't handle non-finite values.
Results may differ from a plain program's by a relative error of at most 0.0003.
Values may be sent and summed in bfloat16 or wider, within the bound.
A program may use at most 64 MiB of HBM per device.

v0:
```python
import math

import jax
import jax.numpy as jnp
from jax import lax
from jax.sharding import PartitionSpec as P

ITERS = 4


def body(worker_feat, firm_feat, worker_pot, firm_pot, worker_caps, firm_caps):
    wfeat = lax.all_gather(worker_feat, "firm", axis=0, tiled=True)
    ffeat = lax.all_gather(firm_feat, "work", axis=0, tiled=True)
    rows_here = wfeat.shape[1]
    cols_here = ffeat.shape[1]
    inverse = 1.0 / (cols_here * lax.axis_size("firm"))
    scale = 1.0 / math.sqrt(wfeat.shape[0])
    width = 256
    blocks = cols_here // width
    first_firm = lax.axis_index("firm") == 0
    first_work = lax.axis_index("work") == 0

    def kernel_pass(vec_u, vec_v):

        def step(rows_acc, index):
            start = index * width
            feat_blk = lax.dynamic_slice_in_dim(ffeat, start, width, 1)
            pot_blk = lax.dynamic_slice_in_dim(firm_pot, start, width, 0)
            vec_blk = lax.dynamic_slice_in_dim(vec_v, start, width, 0)
            surplus = lax.dot_general(
                wfeat, feat_blk, (((0,), (0,)), ((), ())), preferred_element_type=jnp.float32
            )
            kernel = jnp.exp(surplus * scale - worker_pot[:, None] - pot_blk[None, :]) * inverse
            rows_acc = rows_acc + jnp.dot(kernel, vec_blk, precision=lax.Precision.HIGHEST)
            col_blk = jnp.dot(vec_u, kernel, precision=lax.Precision.HIGHEST)
            return (rows_acc, col_blk)

        rows_part, col_blocks = lax.scan(
            step, jnp.zeros((rows_here,), jnp.float32), jnp.arange(blocks, dtype=jnp.int32)
        )
        rows_full = lax.psum(rows_part, "firm")
        cols_part = col_blocks.reshape(cols_here)
        cols = lax.psum(cols_part, "work")
        return (rows_full, cols)

    row_total, col_total = kernel_pass(
        jnp.ones((rows_here,), jnp.float32), jnp.ones((cols_here,), jnp.float32)
    )
    diag_u = row_total + jnp.exp(-worker_pot)
    diag_v = col_total + jnp.exp(-firm_pot)
    rhs_u = diag_u - worker_caps.astype(jnp.float32)
    rhs_v = diag_v - firm_caps.astype(jnp.float32)

    def hessian(dir_u, dir_v):
        prod_u, prod_v = kernel_pass(dir_u, dir_v)
        return (diag_u * dir_u + prod_u, diag_v * dir_v + prod_v)

    def local_dot(left_u, left_v, right_u, right_v):
        part_u = jnp.where(first_firm, jnp.sum(left_u * right_u), 0.0)
        part_v = jnp.where(first_work, jnp.sum(left_v * right_v), 0.0)
        return part_u + part_v

    step_u = jnp.zeros_like(rhs_u)
    step_v = jnp.zeros_like(rhs_v)
    res_u, res_v = (rhs_u, rhs_v)

    def two_products(left_u, left_v, image_u, image_v):
        return lax.psum(
            (
                local_dot(left_u, left_v, left_u, left_v),
                local_dot(left_u, left_v, image_u, image_v),
            ),
            ("work", "firm"),
        )

    image_u, image_v = hessian(res_u, res_v)
    norm_now, product = two_products(res_u, res_v, image_u, image_v)
    alpha = norm_now / product
    dir_u, dir_v = (res_u, res_v)
    along_u, along_v = (image_u, image_v)
    for index in range(ITERS):
        step_u = step_u + alpha * dir_u
        step_v = step_v + alpha * dir_v
        if index + 1 < ITERS:
            res_u = res_u - alpha * along_u
            res_v = res_v - alpha * along_v
            image_u, image_v = hessian(res_u, res_v)
            norm_next, product = two_products(res_u, res_v, image_u, image_v)
            ratio = norm_next / norm_now
            alpha = norm_next / (product - ratio * norm_next / alpha)
            dir_u = res_u + ratio * dir_u
            dir_v = res_v + ratio * dir_v
            along_u = image_u + ratio * along_u
            along_v = image_v + ratio * along_v
            norm_now = norm_next
    return (step_u, step_v)


def solution(mesh):
    placed = (P("firm", "work"), P("work", "firm"), P("work"), P("firm"), P("work"), P("firm"))
    return jax.shard_map(
        body, mesh=mesh, in_specs=placed, out_specs=(P("work"), P("firm")), check_vma=False
    )
```

profile of v0, /device:TPU:0, one launch (start us, length us, event | category | flops | bytes accessed | tf_op | source)
XLA Modules:
  0.0 946.7 jit_solution(16463058012622074813)
XLA Ops:
  0.7 33.2 %all_gather.6 = bf16[64,4096]{1,0:T(8,128)(2,1)S(1)} all-gather(bf16[8,4096]{1,0:T(8,128)(2,1)} %param.17), channel_id=1, replica_groups=mesh['work'=8,'firm'=4] {'work'}, dimensions={0}, use_global_device_ids=true | all-gather | bytes 589824 | tf_op jit(solution)/shard_map/all_gather | solution.py:13
  33.9 6.0 all_gather.7
  39.9 103.3 %while.65 = (s32[]{:T(128)}, f32[2048]{0:T(1024)S(1)}, f32[16,256]{1,0:T(8,128)S(1)}, s32[16]{0:T(128)S(1)}, bf16[64,4096]{1,0:T(8,128)(2,1)S(1)}, /*index=5*/bf...) while((s32[]{:T(128)}, f32[2048]{0:T(1024)S(1)}, ...), condition=%wide.region_1.2_spmd.clone, body=%wide.region_0.1_spmd.clone.sunk | while | flops 81793032 | bytes 6633677 | solution.py:38
  143.2 37.3 %psum.127 = f32[4096]{0:T(1024)S(1)} all-reduce(f32[4096]{0:T(1024)S(1)} %bitcast.176), channel_id=1, replica_groups=mesh['work'=8,'firm'=4] {'work'}, use_global_device_ids=true, to_apply=%region_4.5 | all-reduce | flops 4096 | bytes 32768 | tf_op jit(solution)/shard_map/psum | solution.py:43
  181.2 5.8 psum.126
  187.7 104.5 %while.66 = (s32[]{:T(128)}, f32[2048]{0:T(1024)S(1)}, f32[16,256]{1,0:T(8,128)S(1)}, s32[16]{0:T(128)S(1)}, bf16[64,4096]{1,0:T(8,128)(2,1)S(1)}, /*index=5*/bf...) while((s32[]{:T(128)}, f32[2048]{0:T(1024)S(1)}, ...), condition=%wide.region_8.9_spmd.clone, body=%wide.region_7.8_spmd.clone.sunk | while | flops 81793032 | bytes 6644961 | solution.py:38
  192.4 1.7 fusion.134
  199.0 1.7 fusion.134
  205.5 1.7 fusion.134
  212.0 1.7 fusion.134
  218.5 1.7 fusion.134
  225.1 1.7 fusion.134
  231.6 1.7 fusion.134
  238.1 1.7 fusion.134
  244.7 1.7 fusion.134
  251.2 1.7 fusion.134
  257.7 1.7 fusion.134
  264.2 1.7 fusion.134
  270.8 1.7 fusion.134
  277.3 1.7 fusion.134
  283.8 1.7 fusion.134
  290.4 1.7 fusion.134
  292.1 6.7 psum.129
  300.3 33.0 %psum.130 = f32[4096]{0:T(1024)S(1)} all-reduce(f32[4096]{0:T(1024)S(1)} %bitcast.177), channel_id=1, replica_groups=mesh['work'=8,'firm'=4] {'work'}, use_global_device_ids=true, to_apply=%region_11.12 | all-reduce | flops 4096 | bytes 32768 | tf_op jit(solution)/shard_map/psum | solution.py:43
  335.8 36.9 %all-reduce.3 = (f32[]{:T(128)}, f32[]{:T(128)}) all-reduce(f32[]{:T(128)S(6)} %add.194, f32[]{:T(128)S(6)} %add.197), channel_id=1, replica_groups=mesh['work'=8,'firm'=4] {'work','firm'}, use_global_device_ids=true, to_apply=%region_6.7 | all-reduce | flops 2 | bytes 16 | tf_op jit(solution)/shard_map/psum | solution.py:68
  374.2 101.0 %while.67 = (s32[]{:T(128)}, f32[2048]{0:T(1024)S(1)}, f32[16,256]{1,0:T(8,128)S(1)}, s32[16]{0:T(128)S(1)}, bf16[64,4096]{1,0:T(8,128)(2,1)S(1)}, /*index=5*/bf...) while((s32[]{:T(128)}, f32[2048]{0:T(1024)S(1)}, ...), condition=%wide.region_18.19_spmd.clone, body=%wide.region_17.18_spmd.clone.sunk | while | flops 81793032 | bytes 6644961 | solution.py:38
  378.7 1.7 fusion.143
  385.0 1.7 fusion.143
  391.3 1.7 fusion.143
  397.6 1.7 fusion.143
  403.9 1.7 fusion.143
  410.3 1.7 fusion.143
  416.6 1.7 fusion.143
  422.9 1.7 fusion.143
  429.2 1.7 fusion.143
  435.5 1.7 fusion.143
  441.8 1.7 fusion.143
  448.2 1.7 fusion.143
  454.5 1.7 fusion.143
  460.8 1.7 fusion.143
  467.1 1.7 fusion.143
  473.4 1.7 fusion.143
  475.2 6.4 psum.133
  482.8 36.5 %psum.134 = f32[4096]{0:T(1024)S(1)} all-reduce(f32[4096]{0:T(1024)S(1)} %bitcast.178), channel_id=1, replica_groups=mesh['work'=8,'firm'=4] {'work'}, use_global_device_ids=true, to_apply=%region_21.22 | all-reduce | flops 4096 | bytes 32768 | tf_op jit(solution)/shard_map/psum | solution.py:43
  521.8 36.9 %all-reduce.2 = (f32[]{:T(128)}, f32[]{:T(128)}) all-reduce(f32[]{:T(128)S(6)} %add.198, f32[]{:T(128)S(6)} %add.201), channel_id=1, replica_groups=mesh['work'=8,'firm'=4] {'work','firm'}, use_global_device_ids=true, to_apply=%region_16.17 | all-reduce | flops 2 | bytes 16 | tf_op jit(solution)/shard_map/psum | solution.py:68
  563.2 102.5 %while.68 = (s32[]{:T(128)}, f32[2048]{0:T(1024)S(1)}, f32[16,256]{1,0:T(8,128)S(1)}, s32[16]{0:T(128)S(1)}, bf16[64,4096]{1,0:T(8,128)(2,1)S(1)}, /*index=5*/bf...) while((s32[]{:T(128)}, f32[2048]{0:T(1024)S(1)}, ...), condition=%wide.region_28.29_spmd.clone, body=%wide.region_27.28_spmd.clone.sunk | while | flops 81793032 | bytes 6644961 | solution.py:38
  567.8 1.7 fusion.152
  574.2 1.7 fusion.152
  580.6 1.7 fusion.152
  587.0 1.7 fusion.152
  593.4 1.7 fusion.152
  599.8 1.7 fusion.152
  606.2 1.7 fusion.152
  612.6 1.7 fusion.152
  619.1 1.7 fusion.152
  625.5 1.7 fusion.152
  631.9 1.7 fusion.152
  665.7 6.3 psum.137
  673.3 36.5 %psum.138 = f32[4096]{0:T(1024)S(1)} all-reduce(f32[4096]{0:T(1024)S(1)} %bitcast.179), channel_id=1, replica_groups=mesh['work'=8,'firm'=4] {'work'}, use_global_device_ids=true, to_apply=%region_31.32 | all-reduce | flops 4096 | bytes 32768 | tf_op jit(solution)/shard_map/psum | solution.py:43
  712.5 36.9 %all-reduce.1 = (f32[]{:T(128)}, f32[]{:T(128)}) all-reduce(f32[]{:T(128)S(6)} %add.206, f32[]{:T(128)S(6)} %add.209), channel_id=1, replica_groups=mesh['work'=8,'firm'=4] {'work','firm'}, use_global_device_ids=true, to_apply=%region_26.27 | all-reduce | flops 2 | bytes 16 | tf_op jit(solution)/shard_map/psum | solution.py:68
  753.2 104.5 %while.69 = (s32[]{:T(128)}, f32[2048]{0:T(1024)S(1)}, f32[16,256]{1,0:T(8,128)S(1)}, s32[16]{0:T(128)S(1)}, bf16[64,4096]{1,0:T(8,128)(2,1)S(1)}, /*index=5*/bf...) while((s32[]{:T(128)}, f32[2048]{0:T(1024)S(1)}, ...), condition=%wide.region_38.39_spmd.clone, body=%wide.region_37.38_spmd.clone.sunk | while | flops 81793032 | bytes 6644961 | solution.py:38
  857.7 6.3 psum.141
  865.4 36.5 %psum.142 = f32[4096]{0:T(1024)S(1)} all-reduce(f32[4096]{0:T(1024)S(1)} %bitcast.180), channel_id=1, replica_groups=mesh['work'=8,'firm'=4] {'work'}, use_global_device_ids=true, to_apply=%region_41.42 | all-reduce | flops 4096 | bytes 32768 | tf_op jit(solution)/shard_map/psum | solution.py:43
  904.5 36.9 %all-reduce = (f32[]{:T(128)}, f32[]{:T(128)}) all-reduce(f32[]{:T(128)S(6)} %add.214, f32[]{:T(128)S(6)} %add.217), channel_id=1, replica_groups=mesh['work'=8,'firm'=4] {'work','firm'}, use_global_device_ids=true, to_apply=%region_36.37 | all-reduce | flops 2 | bytes 16 | tf_op jit(solution)/shard_map/psum | solution.py:68
  (623 shorter events, 393.7 us)
Async XLA Ops:
  39.9 140.6 %copy-start = (s32[4096]{0:T(1024)S(1)}, s32[4096]{0:T(1024)}, u32[]{:S(2)}) copy-start(s32[4096]{0:T(1024)} %param.21) | copy-start | bytes 49156
  39.9 147.1 %copy-start.1 = (s32[2048]{0:T(1024)S(1)}, s32[2048]{0:T(1024)}, u32[]{:S(2)}) copy-start(s32[2048]{0:T(1024)} %param.20) | copy-start | bytes 24580
where the time goes:
time: 957 us; the launch traced here: 947 us
  blocking collectives  398 us (42%)
  matrix products  339 us (35%)
  local copies, waits for them, and re-layouts  120 us (13%)
  loops' own time  55.9 us (6%)
  between operations  24.8 us (3%)
    psum x5, blocking collectives, kernel_pass(): cols = lax.psum(cols_part, 'work')  180 us
    psum x4, blocking collectives, two_products(): lax.psum((local_dot(left_u, left_v, left_u, left_v), local_dot(left_u, le...  148 us
    dot_general x80, matrix products, step(): col_blk = jnp.dot(vec_u, kernel, precision=lax.Precision.HIGHEST)  138 us
    dot_general x80, matrix products, step(): lax.dot_general(wfeat, feat_blk, (((0,), (0,)), ((), ())), preferred_elem...  106 us
    dot_general x80, matrix products, step(): jnp.dot(kernel, vec_blk, precision=lax.Precision.HIGHEST)  94.9 us
    dynamic_slice x80, local copies, waits for them, and re-layouts, step(): pot_blk = lax.dynamic_slice_in_dim(firm_pot, start, width, 0)  61.2 us
    another operation x5, loops' own time, kernel_pass(): lax.scan(step, jnp.zeros((rows_here,), jnp.float32), jnp.arange(blocks, d...  55.9 us
    dynamic_slice x80, local copies, waits for them, and re-layouts, kernel_pass(): lax.scan(step, jnp.zeros((rows_here,), jnp.float32), jnp.arange(blocks, d...  50.6 us

commit v1 on v0

v1 whole, which is shorter than its diff:
```python
import functools
import math

import jax
import jax.numpy as jnp
from jax import lax
from jax.experimental import pallas as pl
from jax.experimental.pallas import tpu as pltpu
from jax.sharding import PartitionSpec as P

ITERS = 4
CHUNK = 256
KEEP_BYTES = 40 << 20
MESH = pl.DeviceIdType.MESH


def fold(x):
    total = x[:, 0:128]
    for k in range(1, x.shape[1] // 128):
        total = total + x[:, 128 * k:128 * (k + 1)]
    return total


def kernel(nf, nw, kept, wf_ref, ff_ref, wp_ref, fp_ref, wc_ref, fc_ref, su_ref, sv_ref,
           e_ref, ub, racc, cacc, vb, wt, ft, wslots, fslots, wide_w, wide_f, rows_ref,
           rslots, cslots, sslots, f_send, f_recv, w_send, w_recv, s_send, s_recv):
    R = wf_ref.shape[1]
    C = ff_ref.shape[1]
    feats = wt.shape[1]
    chunks = R // CHUNK
    scale = 1.0 / math.sqrt(feats)
    inverse = 1.0 / (C * nf)
    fi = lax.axis_index("firm")
    wi = lax.axis_index("work")
    W = min(1024, C)
    parts = W // 128

    barrier = pltpu.get_barrier_semaphore()
    for d in range(1, nf):
        pl.semaphore_signal(barrier, 1, device_id={"firm": lax.rem(fi + d, nf)}, device_id_type=MESH)
    for d in range(1, nw):
        pl.semaphore_signal(barrier, 1, device_id={"work": lax.rem(wi + d, nw)}, device_id_type=MESH)
    pl.semaphore_wait(barrier, nf + nw - 2)

    def send_firm(src, dst, stage):
        copies = []
        for d in range(1, nf):
            copy = pltpu.make_async_remote_copy(
                src_ref=src, dst_ref=dst, send_sem=f_send.at[stage, d], recv_sem=f_recv.at[stage, d],
                device_id={"firm": lax.rem(fi + d, nf)}, device_id_type=MESH)
            copy.start()
            copies.append(copy)
        return copies

    def send_work(src, dst, send, recv, stage):
        copies = []
        for d in range(1, nw):
            copy = pltpu.make_async_remote_copy(
                src_ref=src, dst_ref=dst, send_sem=send.at[stage, d], recv_sem=recv.at[stage, d],
                device_id={"work": lax.rem(wi + d, nw)}, device_id_type=MESH)
            copy.start()
            copies.append(copy)
        return copies

    def finish(copies):
        for copy in copies:
            copy.wait()

    g_work = send_work(ff_ref, fslots.at[wi], w_send, w_recv, 0)
    g_firm = send_firm(wf_ref, wslots.at[fi], 0)
    wslots[fi] = wf_ref[...]
    fslots[wi] = ff_ref[...]
    exp_w = jnp.exp(-wp_ref[...])
    exp_f = jnp.exp(-fp_ref[...])
    left = exp_w
    right = exp_f * inverse

    def set_ub(x):
        for k in range(R // 128):
            ub[128 * k:128 * (k + 1), :] = jnp.transpose(
                jnp.broadcast_to(x[:, 128 * k:128 * (k + 1)], (128, 128)))

    def set_vb(y):
        vb[...] = jnp.broadcast_to(y, (8, C))

    set_ub(left)
    set_vb(right)
    finish(g_firm)
    fr = wf_ref.shape[0]
    for k in range(nf):
        wide_w[fr * k:fr * (k + 1), :] = wslots[k].astype(jnp.float32)
    for k in range(R // 128):
        wt[128 * k:128 * (k + 1), :] = jnp.transpose(wide_w[:, 128 * k:128 * (k + 1)]).astype(jnp.bfloat16)
    finish(g_work)
    wr = ff_ref.shape[0]
    for k in range(nw):
        wide_f[wr * k:wr * (k + 1), :] = fslots[k].astype(jnp.float32)
    ft[...] = wide_f[...].astype(jnp.bfloat16)

    def build(row0, slot0):
        for cb in range(C // 512):
            s = jnp.dot(wt[pl.ds(row0, CHUNK), :], ft[:, 512 * cb:512 * (cb + 1)],
                        preferred_element_type=jnp.float32)
            e_ref[pl.ds(slot0, CHUNK), 512 * cb:512 * (cb + 1)] = jnp.exp(s * scale)

    def sweep(row0, slot0, with_cols):
        unroll = 4
        for cb in range(C // W):
            base = cb * W
            vecs = [vb[:, base + 128 * j:base + 128 * (j + 1)] for j in range(parts)]

            def step(g, accs):
                accs = list(accs)
                for k in range(unroll):
                    off = pl.multiple_of(g * (8 * unroll), 8 * unroll) + 8 * k
                    src = pl.multiple_of(slot0 + off, 8)
                    row = pl.multiple_of(row0 + off, 8)
                    u = ub[pl.ds(row, 8), :]
                    total = racc[pl.ds(row, 8), :]
                    for j in range(parts):
                        e = e_ref[pl.ds(src, 8), base + 128 * j:base + 128 * (j + 1)]
                        total = total + e * vecs[j]
                        if with_cols:
                            accs[j] = accs[j] + e * u
                    racc[pl.ds(row, 8), :] = total
                return tuple(accs)

            init = ()
            if with_cols:
                init = tuple(cacc[:, base + 128 * j:base + 128 * (j + 1)] for j in range(parts))
            accs = lax.fori_loop(0, CHUNK // (8 * unroll), step, init)
            if with_cols:
                for j in range(parts):
                    cacc[:, base + 128 * j:base + 128 * (j + 1)] = accs[j]

    def kernel_pass(first, with_cols):
        racc[...] = jnp.zeros_like(racc)
        if with_cols:
            cacc[...] = jnp.zeros_like(cacc)

        def held(c, _):
            row0 = pl.multiple_of(c * CHUNK, CHUNK)
            if first:
                build(row0, row0)
            sweep(row0, row0, with_cols)
            return 0

        lax.fori_loop(0, kept, held, 0)
        if kept < chunks:
            def rest(c, _):
                row0 = pl.multiple_of(c * CHUNK, CHUNK)
                build(row0, kept * CHUNK)
                sweep(row0, kept * CHUNK, with_cols)
                return 0

            lax.fori_loop(kept, chunks, rest, 0)

    def row_part():
        for k in range(R // 128):
            block = jnp.transpose(racc[128 * k:128 * (k + 1), :])
            rows_ref[:, 128 * k:128 * (k + 1)] = jnp.sum(block, axis=0, keepdims=True)
        return rows_ref[...] * left

    def col_part():
        return jnp.sum(cacc[...], axis=0, keepdims=True) * right

    def total_of(ref, stage, n, cut):
        total = ref[stage, 0, :, cut]
        for k in range(1, n):
            total = total + ref[stage, k, :, cut]
        return total

    rows_cut = slice(0, R)
    dots_cut = slice(R, R + 256)

    def send_cols(stage):
        cslots[stage, wi] = col_part()
        return send_work(cslots.at[stage, wi], cslots.at[stage, wi], w_send, w_recv, stage + 1)

    kernel_pass(True, True)
    c_copies = send_cols(0)
    rslots[0, fi, :, rows_cut] = row_part()
    r_copies = send_firm(rslots.at[0, fi, :, rows_cut], rslots.at[0, fi, :, rows_cut], 1)
    finish(r_copies)
    diag_u = total_of(rslots, 0, nf, rows_cut) + exp_w
    finish(c_copies)
    diag_v = total_of(cslots, 0, nw, slice(0, C)) + exp_f
    res_u = diag_u - wc_ref[...].astype(jnp.float32)
    res_v = diag_v - fc_ref[...].astype(jnp.float32)

    count_u = jnp.where(fi == 0, 1.0, 0.0)
    count_v = jnp.where(wi == 0, 1.0, 0.0)
    dir_u = dir_v = along_u = along_v = step_u = step_v = None
    norm_now = alpha = None
    for index in range(ITERS):
        last = index + 1 == ITERS
        stage = index + 1
        set_ub(res_u * left)
        set_vb(res_v * right)
        kernel_pass(False, not last)
        sq_u = res_u * res_u
        sq_v = res_v * res_v
        norms = fold(sq_u) * count_u + fold(sq_v) * count_v
        diags = fold(diag_u * sq_u) * count_u + fold(diag_v * sq_v) * count_v
        if not last:
            c_copies = send_cols(stage)
            part = row_part()
            rslots[stage, fi, :, rows_cut] = part
            cross = fold(part * res_u)
            sent = slice(0, R + 256)
        else:
            cross = jnp.sum(racc[...] * ub[...], axis=0, keepdims=True)
            sent = dots_cut
        rslots[stage, fi, :, slice(R, R + 128)] = norms
        rslots[stage, fi, :, slice(R + 128, R + 256)] = diags + 2.0 * cross
        r_copies = send_firm(rslots.at[stage, fi, :, sent], rslots.at[stage, fi, :, sent], stage + 1)
        finish(r_copies)
        sslots[index, wi] = total_of(rslots, stage, nf, dots_cut)
        s_copies = send_work(sslots.at[index, wi], sslots.at[index, wi], s_send, s_recv, index)
        if not last:
            image_u = diag_u * res_u + total_of(rslots, stage, nf, rows_cut)
            finish(c_copies)
            image_v = diag_v * res_v + total_of(cslots, stage, nw, slice(0, C))
        finish(s_copies)
        dots = total_of(sslots, index, nw, slice(0, 256))
        norm_next = jnp.sum(dots[:, 0:128], axis=1, keepdims=True)
        product = jnp.sum(dots[:, 128:256], axis=1, keepdims=True)
        if index == 0:
            alpha = norm_next / product
            dir_u, dir_v = res_u, res_v
            step_u, step_v = alpha * dir_u, alpha * dir_v
            along_u, along_v = image_u, image_v
        else:
            ratio = norm_next / norm_now
            alpha = norm_next / (product - ratio * norm_next / alpha)
            dir_u = res_u + ratio * dir_u
            dir_v = res_v + ratio * dir_v
            step_u = step_u + alpha * dir_u
            step_v = step_v + alpha * dir_v
            if not last:
                along_u = image_u + ratio * along_u
                along_v = image_v + ratio * along_v
        if not last:
            res_u = res_u - alpha * along_u
            res_v = res_v - alpha * along_v
        norm_now = norm_next
    su_ref[...] = step_u
    sv_ref[...] = step_v


def body(worker_feat, firm_feat, worker_pot, firm_pot, worker_caps, firm_caps):
    nf = lax.axis_size("firm")
    nw = lax.axis_size("work")
    fr, R = worker_feat.shape
    wr, C = firm_feat.shape
    feats = fr * nf
    chunks = R // CHUNK
    kept = min(chunks, KEEP_BYTES // (CHUNK * C * 4))
    held_rows = (kept if kept == chunks else kept + 1) * CHUNK
    f32 = jnp.float32
    dma = pltpu.SemaphoreType.DMA
    vmem = pl.BlockSpec(memory_space=pltpu.VMEM)
    su, sv = pl.pallas_call(
        functools.partial(kernel, nf, nw, kept),
        out_shape=(jax.ShapeDtypeStruct((1, R), f32), jax.ShapeDtypeStruct((1, C), f32)),
        in_specs=[vmem] * 6,
        out_specs=(vmem, vmem),
        scratch_shapes=[
            pltpu.VMEM((held_rows, C), f32),
            pltpu.VMEM((R, 128), f32),
            pltpu.VMEM((R, 128), f32),
            pltpu.VMEM((8, C), f32),
            pltpu.VMEM((8, C), f32),
            pltpu.VMEM((R, feats), jnp.bfloat16),
            pltpu.VMEM((feats, C), jnp.bfloat16),
            pltpu.VMEM((nf, fr, R), jnp.bfloat16),
            pltpu.VMEM((nw, wr, C), jnp.bfloat16),
            pltpu.VMEM((feats, R), f32),
            pltpu.VMEM((feats, C), f32),
            pltpu.VMEM((1, R), f32),
            pltpu.VMEM((ITERS + 1, nf, 1, R + 256), f32),
            pltpu.VMEM((ITERS, nw, 1, C), f32),
            pltpu.VMEM((ITERS, nw, 1, 256), f32),
            dma((ITERS + 2, nf)), dma((ITERS + 2, nf)),
            dma((ITERS + 1, nw)), dma((ITERS + 1, nw)),
            dma((ITERS, nw)), dma((ITERS, nw)),
        ],
        compiler_params=pltpu.CompilerParams(
            collective_id=0, has_side_effects=True, vmem_limit_bytes=60 << 20),
    )(worker_feat, firm_feat, worker_pot[None, :], firm_pot[None, :],
      worker_caps[None, :], firm_caps[None, :])
    return su.reshape(R), sv.reshape(C)


def solution(mesh):
    placed = (P("firm", "work"), P("work", "firm"), P("work"), P("firm"), P("work"), P("firm"))
    return jax.shard_map(
        body, mesh=mesh, in_specs=placed, out_specs=(P("work"), P("firm")), check_vma=False
    )
```

time: 957 us -> 95.4 us (0.10); the launches traced: 947 us -> 95.2 us
  blocking collectives: 398 us -> 0 us
  matrix products: 339 us -> 0 us
  local copies, waits for them, and re-layouts: 120 us -> 1.91 us
  Pallas kernels: 0 us -> 92.7 us
  loops' own time: 55.9 us -> 0 us
  between operations: 24.8 us -> 0.65 us
    psum x14 -> x0, blocking collectives: 359 us -> none  [the longest x5 180 us: kernel_pass(): cols = lax.psum(cols_part, 'work')]
    dot_general x240 -> x0, matrix products: 339 us -> none  [the longest x80 138 us: step(): col_blk = jnp.dot(vec_u, kernel, precision=lax.Precision.HIGHEST)]
    dynamic_slice x224 -> x0, local copies, waits for them, and re-layouts: 117 us -> none  [the longest x80 61.2 us: step(): pot_blk = lax.dynamic_slice_in_dim(firm_pot, start, width, 0)]
    pallas_call x0 -> x1, Pallas kernels: none -> 92.7 us  [body(): pl.pallas_call(functools.partial(kernel, nf, nw, kept), out_shape=(jax.Sh...]
    another operation x5 -> x0, loops' own time: 55.9 us -> none  [kernel_pass(): lax.scan(step, jnp.zeros((rows_here,), jnp.float32), jnp.arange(blocks, d...]
    all_gather x2 -> x0, blocking collectives: 39.2 us -> none  [the longest x1 33.2 us: body(): ffeat = lax.all_gather(firm_feat, 'work', axis=0, tiled=True)]
where the time goes in v1:
time: 95.4 us; the launch traced here: 95.2 us
  Pallas kernels  92.7 us (97%)
  local copies, waits for them, and re-layouts  1.91 us (2%)
    pallas_call x1, Pallas kernels, body(): pl.pallas_call(functools.partial(kernel, nf, nw, kept), out_shape=(jax.Sh...  92.7 us
    unnamed x4, local copies, waits for them, and re-layouts  1.91 us

profile of v1, /device:TPU:0, one launch (start us, length us, event | category | flops | bytes accessed | tf_op | source)
XLA Modules:
  0.0 95.2 jit_solution(17693521777729333473)
XLA Ops:
  0.6 92.7 %shard_map.77 = (f32[1,2048]{1,0:T(1,128)}, f32[1,4096]{1,0:T(1,128)}) custom-call(bf16[16,2048]{1,0:T(8,128)(2,1)} %wf_ref.1, bf16[8,4096]{1,0:T(8,128)(2,1)} %ff_ref.1, f32[1,2048]{1,0:T(1,128)} %bitcast.9, f32[1,4096]{1,0:T(1,128)} %bitcast.7, s32[1,2048]{1,0:T(1,128)} %bitcast.10, s32[1,4096]{1,0:T(1,128)} %bitcast.8), custom_call_target="tpu_custom_call" | custom-call | tf_op jit(solution)/shard_map/pallas_call | solution.py:263
  93.3 0.0 copy-start
  93.3 1.3 %copy.10 = f32[2048]{0:T(1024)} copy(f32[2048]{0:T(1024)} %bitcast.11) | data formatting | bytes 16384
  94.6 0.0 copy-done
  94.6 0.6 copy.11
Async XLA Ops:
  93.3 1.3 %copy-start = (f32[1,4096]{1,0:T(1,128)S(1)}, f32[1,4096]{1,0:T(1,128)}, u32[]{:S(2)}) copy-start(f32[1,4096]{1,0:T(1,128)} %get-tuple-element.5) | copy-start | bytes 49156

commit v2 on v1

--- a/solution.py
+++ b/solution.py
@@ -23,7 +23,7 @@
 
 def kernel(nf, nw, kept, wf_ref, ff_ref, wp_ref, fp_ref, wc_ref, fc_ref, su_ref, sv_ref,
            e_ref, ub, racc, cacc, vb, wt, ft, wslots, fslots, wide_w, wide_f, rows_ref,
-           rslots, cslots, sslots, f_send, f_recv, w_send, w_recv, s_send, s_recv):
+           rslots, cslots, sslots, f_send, f_recv, w_send, w_recv, s_send, s_recv, g_send, g_recv):
     R = wf_ref.shape[1]
     C = ff_ref.shape[1]
     feats = wt.shape[1]
@@ -66,8 +66,16 @@
         for copy in copies:
             copy.wait()
 
-    g_work = send_work(ff_ref, fslots.at[wi], w_send, w_recv, 0)
     g_firm = send_firm(wf_ref, wslots.at[fi], 0)
+    g_work = []
+
+    def send_piece():
+        cb = len(g_work)
+        if cb < C // W:
+            span = slice(W * cb, W * (cb + 1))
+            g_work.append(send_work(ff_ref.at[:, span], fslots.at[wi, :, span], g_send, g_recv, cb))
+
+    send_piece()
     wslots[fi] = wf_ref[...]
     fslots[wi] = ff_ref[...]
     exp_w = jnp.exp(-wp_ref[...])
@@ -91,21 +99,28 @@
         wide_w[fr * k:fr * (k + 1), :] = wslots[k].astype(jnp.float32)
     for k in range(R // 128):
         wt[128 * k:128 * (k + 1), :] = jnp.transpose(wide_w[:, 128 * k:128 * (k + 1)]).astype(jnp.bfloat16)
-    finish(g_work)
     wr = ff_ref.shape[0]
-    for k in range(nw):
-        wide_f[wr * k:wr * (k + 1), :] = fslots[k].astype(jnp.float32)
-    ft[...] = wide_f[...].astype(jnp.bfloat16)
-
-    def build(row0, slot0):
-        for cb in range(C // 512):
+
+    def arrive(cb):
+        span = slice(W * cb, W * (cb + 1))
+        for copy in g_work[cb]:
+            copy.wait_send()
+        send_piece()
+        for copy in g_work[cb]:
+            copy.wait_recv()
+        for k in range(nw):
+            wide_f[wr * k:wr * (k + 1), span] = fslots[k, :, span].astype(jnp.float32)
+        ft[:, span] = wide_f[:, span].astype(jnp.bfloat16)
+
+    def build(row0, slot0, spans):
+        for cb in spans:
             s = jnp.dot(wt[pl.ds(row0, CHUNK), :], ft[:, 512 * cb:512 * (cb + 1)],
                         preferred_element_type=jnp.float32)
             e_ref[pl.ds(slot0, CHUNK), 512 * cb:512 * (cb + 1)] = jnp.exp(s * scale)
 
-    def sweep(row0, slot0, with_cols):
-        unroll = 4
-        for cb in range(C // W):
+    def sweep(row0, slot0, with_cols, spans):
+        unroll = CHUNK // 8
+        for cb in spans:
             base = cb * W
             vecs = [vb[:, base + 128 * j:base + 128 * (j + 1)] for j in range(parts)]
 
@@ -138,22 +153,32 @@
         if with_cols:
             cacc[...] = jnp.zeros_like(cacc)
 
-        def held(c, _):
-            row0 = pl.multiple_of(c * CHUNK, CHUNK)
-            if first:
-                build(row0, row0)
-            sweep(row0, row0, with_cols)
-            return 0
-
-        lax.fori_loop(0, kept, held, 0)
-        if kept < chunks:
+        def both(spans, fresh):
+            cuts = [k for cb in spans for k in range(cb * W // 512, (cb + 1) * W // 512)]
+
+            def held(c, _):
+                row0 = pl.multiple_of(c * CHUNK, CHUNK)
+                if fresh:
+                    build(row0, row0, cuts)
+                sweep(row0, row0, with_cols, spans)
+                return 0
+
             def rest(c, _):
                 row0 = pl.multiple_of(c * CHUNK, CHUNK)
-                build(row0, kept * CHUNK)
-                sweep(row0, kept * CHUNK, with_cols)
+                build(row0, kept * CHUNK, cuts)
+                sweep(row0, kept * CHUNK, with_cols, spans)
                 return 0
 
-            lax.fori_loop(kept, chunks, rest, 0)
+            lax.fori_loop(0, kept, held, 0)
+            if kept < chunks:
+                lax.fori_loop(kept, chunks, rest, 0)
+
+        if first:
+            for cb in range(C // W):
+                arrive(cb)
+                both([cb], True)
+        else:
+            both(list(range(C // W)), False)
 
     def row_part():
         for k in range(R // 128):
@@ -173,12 +198,12 @@
     rows_cut = slice(0, R)
     dots_cut = slice(R, R + 256)
 
-    def send_cols(stage):
-        cslots[stage, wi] = col_part()
+    def send_cols(stage, part):
+        cslots[stage, wi] = part
         return send_work(cslots.at[stage, wi], cslots.at[stage, wi], w_send, w_recv, stage + 1)
 
     kernel_pass(True, True)
-    c_copies = send_cols(0)
+    c_copies = send_cols(0, col_part())
     rslots[0, fi, :, rows_cut] = row_part()
     r_copies = send_firm(rslots.at[0, fi, :, rows_cut], rslots.at[0, fi, :, rows_cut], 1)
     finish(r_copies)
@@ -190,46 +215,53 @@
 
     count_u = jnp.where(fi == 0, 1.0, 0.0)
     count_v = jnp.where(wi == 0, 1.0, 0.0)
-    dir_u = dir_v = along_u = along_v = step_u = step_v = None
+    set_ub(res_u * left)
+    set_vb(res_v * right)
+    kernel_pass(False, True)
+    part_v = col_part()
+    part_u = row_part()
+    dir_u = dir_v = along_u = along_v = step_u = step_v = acc_u = acc_v = None
     norm_now = alpha = None
     for index in range(ITERS):
         last = index + 1 == ITERS
         stage = index + 1
-        set_ub(res_u * left)
-        set_vb(res_v * right)
-        kernel_pass(False, not last)
+        if not last:
+            c_copies = send_cols(stage, part_v)
+            rslots[stage, fi, :, rows_cut] = part_u
+        sent = dots_cut if last else slice(0, R + 256)
         sq_u = res_u * res_u
         sq_v = res_v * res_v
         norms = fold(sq_u) * count_u + fold(sq_v) * count_v
         diags = fold(diag_u * sq_u) * count_u + fold(diag_v * sq_v) * count_v
-        if not last:
-            c_copies = send_cols(stage)
-            part = row_part()
-            rslots[stage, fi, :, rows_cut] = part
-            cross = fold(part * res_u)
-            sent = slice(0, R + 256)
-        else:
-            cross = jnp.sum(racc[...] * ub[...], axis=0, keepdims=True)
-            sent = dots_cut
         rslots[stage, fi, :, slice(R, R + 128)] = norms
-        rslots[stage, fi, :, slice(R + 128, R + 256)] = diags + 2.0 * cross
+        rslots[stage, fi, :, slice(R + 128, R + 256)] = diags + 2.0 * fold(part_u * res_u)
         r_copies = send_firm(rslots.at[stage, fi, :, sent], rslots.at[stage, fi, :, sent], stage + 1)
         finish(r_copies)
-        sslots[index, wi] = total_of(rslots, stage, nf, dots_cut)
+        both_dots = total_of(rslots, stage, nf, dots_cut)
+        sslots[index, wi, 0:1, :] = both_dots[:, 0:128]
+        sslots[index, wi, 1:2, :] = both_dots[:, 128:256]
         s_copies = send_work(sslots.at[index, wi], sslots.at[index, wi], s_send, s_recv, index)
         if not last:
             image_u = diag_u * res_u + total_of(rslots, stage, nf, rows_cut)
+            set_ub(image_u * left)
             finish(c_copies)
             image_v = diag_v * res_v + total_of(cslots, stage, nw, slice(0, C))
+            set_vb(image_v * right)
+            kernel_pass(False, index + 2 < ITERS)
+            prod_u = row_part()
+            prod_v = col_part() if index + 2 < ITERS else None
         finish(s_copies)
-        dots = total_of(sslots, index, nw, slice(0, 256))
-        norm_next = jnp.sum(dots[:, 0:128], axis=1, keepdims=True)
-        product = jnp.sum(dots[:, 128:256], axis=1, keepdims=True)
+        dots = sslots[index, 0]
+        for k in range(1, nw):
+            dots = dots + sslots[index, k]
+        norm_next = jnp.sum(dots[0:1, :], axis=1, keepdims=True)
+        product = jnp.sum(dots[1:2, :], axis=1, keepdims=True)
         if index == 0:
             alpha = norm_next / product
             dir_u, dir_v = res_u, res_v
             step_u, step_v = alpha * dir_u, alpha * dir_v
             along_u, along_v = image_u, image_v
+            acc_u, acc_v = prod_u, prod_v
         else:
             ratio = norm_next / norm_now
             alpha = norm_next / (product - ratio * norm_next / alpha)
@@ -240,9 +272,15 @@
             if not last:
                 along_u = image_u + ratio * along_u
                 along_v = image_v + ratio * along_v
+                acc_u = prod_u + ratio * acc_u
+                if prod_v is not None:
+                    acc_v = prod_v + ratio * acc_v
         if not last:
             res_u = res_u - alpha * along_u
             res_v = res_v - alpha * along_v
+            part_u = part_u - alpha * acc_u
+            if prod_v is not None:
+                part_v = part_v - alpha * acc_v
         norm_now = norm_next
     su_ref[...] = step_u
     sv_ref[...] = step_v
@@ -257,6 +295,7 @@
     chunks = R // CHUNK
     kept = min(chunks, KEEP_BYTES // (CHUNK * C * 4))
     held_rows = (kept if kept == chunks else kept + 1) * CHUNK
+    pieces = C // min(1024, C)
     f32 = jnp.float32
     dma = pltpu.SemaphoreType.DMA
     vmem = pl.BlockSpec(memory_space=pltpu.VMEM)
@@ -280,10 +319,11 @@
             pltpu.VMEM((1, R), f32),
             pltpu.VMEM((ITERS + 1, nf, 1, R + 256), f32),
             pltpu.VMEM((ITERS, nw, 1, C), f32),
-            pltpu.VMEM((ITERS, nw, 1, 256), f32),
+            pltpu.VMEM((ITERS, nw, 2, 128), f32),
             dma((ITERS + 2, nf)), dma((ITERS + 2, nf)),
             dma((ITERS + 1, nw)), dma((ITERS + 1, nw)),
             dma((ITERS, nw)), dma((ITERS, nw)),
+            dma((pieces, nw)), dma((pieces, nw)),
         ],
         compiler_params=pltpu.CompilerParams(
             collective_id=0, has_side_effects=True, vmem_limit_bytes=60 << 20),

time: 95.4 us -> 76.5 us (0.80)
  Pallas kernels: 92.7 us -> 73.7 us
    pallas_call x1, Pallas kernels: 92.7 us -> 73.7 us  [body(): pl.pallas_call(functools.partial(kernel, nf, nw, kept), out_shape=(jax.Sh...]
where the time goes in v2:
time: 76.5 us; the launch traced here: 76.3 us
  Pallas kernels  73.7 us (96%)
  local copies, waits for them, and re-layouts  1.91 us (2%)
    pallas_call x1, Pallas kernels, body(): pl.pallas_call(functools.partial(kernel, nf, nw, kept), out_shape=(jax.Sh...  73.7 us
    unnamed x4, local copies, waits for them, and re-layouts  1.91 us

profile of v2, /device:TPU:0, one launch (start us, length us, event | category | flops | bytes accessed | tf_op | source)
XLA Modules:
  0.0 76.3 jit_solution(3298032542370392408)
XLA Ops:
  0.6 73.7 %shard_map.77 = (f32[1,2048]{1,0:T(1,128)}, f32[1,4096]{1,0:T(1,128)}) custom-call(bf16[16,2048]{1,0:T(8,128)(2,1)} %wf_ref.1, bf16[8,4096]{1,0:T(8,128)(2,1)} %ff_ref.1, f32[1,2048]{1,0:T(1,128)} %bitcast.9, f32[1,4096]{1,0:T(1,128)} %bitcast.7, s32[1,2048]{1,0:T(1,128)} %bitcast.10, s32[1,4096]{1,0:T(1,128)} %bitcast.8), custom_call_target="tpu_custom_call" | custom-call | tf_op jit(solution)/shard_map/pallas_call | solution.py:302
  74.4 0.0 copy-start
  74.4 1.3 %copy.10 = f32[2048]{0:T(1024)} copy(f32[2048]{0:T(1024)} %bitcast.11) | data formatting | bytes 16384
  75.7 0.0 copy-done
  75.7 0.6 copy.11
Async XLA Ops:
  74.4 1.3 %copy-start = (f32[1,4096]{1,0:T(1,128)S(1)}, f32[1,4096]{1,0:T(1,128)}, u32[]{:S(2)}) copy-start(f32[1,4096]{1,0:T(1,128)} %get-tuple-element.5) | copy-start | bytes 49156

commit v3 on v2

--- a/solution.py
+++ b/solution.py
@@ -116,7 +116,7 @@
         for cb in spans:
             s = jnp.dot(wt[pl.ds(row0, CHUNK), :], ft[:, 512 * cb:512 * (cb + 1)],
                         preferred_element_type=jnp.float32)
-            e_ref[pl.ds(slot0, CHUNK), 512 * cb:512 * (cb + 1)] = jnp.exp(s * scale)
+            e_ref[pl.ds(slot0, CHUNK), 512 * cb:512 * (cb + 1)] = jnp.exp2(s * (scale * math.log2(math.e)))
 
     def sweep(row0, slot0, with_cols, spans):
         unroll = CHUNK // 8
@@ -148,7 +148,12 @@
                 for j in range(parts):
                     cacc[:, base + 128 * j:base + 128 * (j + 1)] = accs[j]
 
-    def kernel_pass(first, with_cols):
+    blocks = C // W
+    ends = [blocks // 2, blocks] if blocks > 1 else [blocks]
+
+    def kernel_pass(first, cols_stage):
+        with_cols = cols_stage is not None
+        copies = []
         racc[...] = jnp.zeros_like(racc)
         if with_cols:
             cacc[...] = jnp.zeros_like(cacc)
@@ -173,12 +178,22 @@
             if kept < chunks:
                 lax.fori_loop(kept, chunks, rest, 0)
 
-        if first:
-            for cb in range(C // W):
-                arrive(cb)
-                both([cb], True)
-        else:
-            both(list(range(C // W)), False)
+        begin = 0
+        for part, end in enumerate(ends):
+            if first:
+                for cb in range(begin, end):
+                    arrive(cb)
+                    both([cb], True)
+            else:
+                both(list(range(begin, end)), False)
+            if with_cols:
+                span = slice(begin * W, end * W)
+                cslots[cols_stage, wi, :, span] = (
+                    jnp.sum(cacc[:, span], axis=0, keepdims=True) * right[:, span])
+                mine = cslots.at[cols_stage, wi, :, span]
+                copies += send_work(mine, mine, w_send, w_recv, 2 * cols_stage + part)
+            begin = end
+        return copies
 
     def row_part():
         for k in range(R // 128):
@@ -186,9 +201,6 @@
             rows_ref[:, 128 * k:128 * (k + 1)] = jnp.sum(block, axis=0, keepdims=True)
         return rows_ref[...] * left
 
-    def col_part():
-        return jnp.sum(cacc[...], axis=0, keepdims=True) * right
-
     def total_of(ref, stage, n, cut):
         total = ref[stage, 0, :, cut]
         for k in range(1, n):
@@ -198,12 +210,7 @@
     rows_cut = slice(0, R)
     dots_cut = slice(R, R + 256)
 
-    def send_cols(stage, part):
-        cslots[stage, wi] = part
-        return send_work(cslots.at[stage, wi], cslots.at[stage, wi], w_send, w_recv, stage + 1)
-
-    kernel_pass(True, True)
-    c_copies = send_cols(0, col_part())
+    c_copies = kernel_pass(True, 0)
     rslots[0, fi, :, rows_cut] = row_part()
     r_copies = send_firm(rslots.at[0, fi, :, rows_cut], rslots.at[0, fi, :, rows_cut], 1)
     finish(r_copies)
@@ -217,16 +224,14 @@
     count_v = jnp.where(wi == 0, 1.0, 0.0)
     set_ub(res_u * left)
     set_vb(res_v * right)
-    kernel_pass(False, True)
-    part_v = col_part()
+    c_copies = kernel_pass(False, 1)
     part_u = row_part()
-    dir_u = dir_v = along_u = along_v = step_u = step_v = acc_u = acc_v = None
+    dir_u = dir_v = along_u = along_v = step_u = step_v = acc_u = acc_v = full_v = ratio = None
     norm_now = alpha = None
     for index in range(ITERS):
         last = index + 1 == ITERS
         stage = index + 1
         if not last:
-            c_copies = send_cols(stage, part_v)
             rslots[stage, fi, :, rows_cut] = part_u
         sent = dots_cut if last else slice(0, R + 256)
         sq_u = res_u * res_u
@@ -245,11 +250,16 @@
             image_u = diag_u * res_u + total_of(rslots, stage, nf, rows_cut)
             set_ub(image_u * left)
             finish(c_copies)
-            image_v = diag_v * res_v + total_of(cslots, stage, nw, slice(0, C))
+            got = total_of(cslots, stage, nw, slice(0, C))
+            if index == 0:
+                full_v = got
+            else:
+                acc_v = got if index == 1 else got + ratio * acc_v
+                full_v = full_v - alpha * acc_v
+            image_v = diag_v * res_v + full_v
             set_vb(image_v * right)
-            kernel_pass(False, index + 2 < ITERS)
+            c_copies = kernel_pass(False, index + 2 if index + 2 < ITERS else None)
             prod_u = row_part()
-            prod_v = col_part() if index + 2 < ITERS else None
         finish(s_copies)
         dots = sslots[index, 0]
         for k in range(1, nw):
@@ -261,7 +271,7 @@
             dir_u, dir_v = res_u, res_v
             step_u, step_v = alpha * dir_u, alpha * dir_v
             along_u, along_v = image_u, image_v
-            acc_u, acc_v = prod_u, prod_v
+            acc_u = prod_u
         else:
             ratio = norm_next / norm_now
             alpha = norm_next / (product - ratio * norm_next / alpha)
@@ -273,14 +283,10 @@
                 along_u = image_u + ratio * along_u
                 along_v = image_v + ratio * along_v
                 acc_u = prod_u + ratio * acc_u
-                if prod_v is not None:
-                    acc_v = prod_v + ratio * acc_v
         if not last:
             res_u = res_u - alpha * along_u
             res_v = res_v - alpha * along_v
             part_u = part_u - alpha * acc_u
-            if prod_v is not None:
-                part_v = part_v - alpha * acc_v
         norm_now = norm_next
     su_ref[...] = step_u
     sv_ref[...] = step_v
@@ -321,7 +327,7 @@
             pltpu.VMEM((ITERS, nw, 1, C), f32),
             pltpu.VMEM((ITERS, nw, 2, 128), f32),
             dma((ITERS + 2, nf)), dma((ITERS + 2, nf)),
-            dma((ITERS + 1, nw)), dma((ITERS + 1, nw)),
+            dma((2 * ITERS, nw)), dma((2 * ITERS, nw)),
             dma((ITERS, nw)), dma((ITERS, nw)),
             dma((pieces, nw)), dma((pieces, nw)),
         ],

time: 76.5 us -> 75.9 us (level)
  no operation moved by 1% of the time
where the time goes in v3:
time: 75.9 us; the launch traced here: 75.7 us
  Pallas kernels  73.1 us (96%)
  local copies, waits for them, and re-layouts  1.91 us (3%)
    pallas_call x1, Pallas kernels, body(): pl.pallas_call(functools.partial(kernel, nf, nw, kept), out_shape=(jax.Sh...  73.1 us
    unnamed x4, local copies, waits for them, and re-layouts  1.91 us

profile of v3, /device:TPU:0, one launch (start us, length us, event | category | flops | bytes accessed | tf_op | source)
XLA Modules:
  0.0 75.7 jit_solution(15788812715728323583)
XLA Ops:
  0.6 73.1 %shard_map.77 = (f32[1,2048]{1,0:T(1,128)}, f32[1,4096]{1,0:T(1,128)}) custom-call(bf16[16,2048]{1,0:T(8,128)(2,1)} %wf_ref.1, bf16[8,4096]{1,0:T(8,128)(2,1)} %ff_ref.1, f32[1,2048]{1,0:T(1,128)} %bitcast.9, f32[1,4096]{1,0:T(1,128)} %bitcast.7, s32[1,2048]{1,0:T(1,128)} %bitcast.10, s32[1,4096]{1,0:T(1,128)} %bitcast.8), custom_call_target="tpu_custom_call" | custom-call | tf_op jit(solution)/shard_map/pallas_call | solution.py:308
  73.8 0.0 copy-start
  73.8 1.3 %copy.10 = f32[2048]{0:T(1024)} copy(f32[2048]{0:T(1024)} %bitcast.11) | data formatting | bytes 16384
  75.1 0.0 copy-done
  75.1 0.6 copy.11
Async XLA Ops:
  73.8 1.3 %copy-start = (f32[1,4096]{1,0:T(1,128)S(1)}, f32[1,4096]{1,0:T(1,128)}, u32[]{:S(2)}) copy-start(f32[1,4096]{1,0:T(1,128)} %get-tuple-element.5) | copy-start | bytes 49156
